TPU v7x, 32 devices: a whole 2x2x4 slice. The times are simulated.
32 devices in a mesh: row: 4 (over y, core), col: 8 (over z, x).
Axes of the slice: x: 2, y: 2, z: 4, core: 2. Of those that a mesh axis runs over, the one named last changes fastest.
Arguments:
- kernels: bfloat16 [6, 4096, 6144], P(None, 'col', 'row'), may hold values from -0.03125 to 0.03125
- history: bfloat16 [6, 6144, 256], P(None, ('row', 'col')), may hold values from -6 to 6
- incident: float32 [32, 128, 256], P(('row', 'col')), may hold values from -6 to 6
- owner: int32 [32], replicated, may hold values from 0 to 3, as said below
- tile_pairs: int32 [384, 2], P(('row', 'col')), may hold values from 0 to 31, as said below
- tile_values: bfloat16 [384, 128, 128], P(('row', 'col')), may hold values from -0.109375 to 0.109375
- tile_counts: int32 [32], P(('row', 'col')), may hold values from 1 to 12, as said below
Outputs:
- density: float32 [32, 128, 256], P(('row', 'col'))
Inputs may be any that keep to these rules, and one draw needn't show every extreme that they name: `owner`: within each block of 4 consecutive clusters starting at a multiple of 4, the owners are all different. tile_pairs[t, 0] is the cluster whose slot is t // 12; for a target cluster k the sources of its slot are distinct clusters whose block (cluster // 4) is k // 4 - 1, k // 4 or k // 4 + 1, modulo 8. `tile_counts`: some device has all 12 slots live.
All inputs are finite; a program needn't handle non-finite values.
Results may differ from a plain program's by a relative error of at most 0.0012.
Values may be sent and summed in bfloat16 or wider, within the bound.
No kernel may reach another device: no remote copies, remote signals or barrier semaphores. Data moves between devices by JAX's collectives and lax.ppermute only.
A program may use at most 128 MiB of HBM per device.

v0:
```python
import jax
import jax.numpy as jnp
from jax import lax
from jax.sharding import PartitionSpec as P

SWEEPS = 3
damping = 0.7


def with_halo(cells, sides, width):
    for axis, dim in sides:
        count = lax.axis_size(axis)
        head = lax.slice_in_dim(cells, 0, width, axis=dim)
        tail = lax.slice_in_dim(cells, cells.shape[dim] - width, cells.shape[dim], axis=dim)
        cells = jnp.concatenate(
            [
                lax.ppermute(tail, axis, [(i, (i + 1) % count) for i in range(count)]),
                cells,
                lax.ppermute(head, axis, [((i + 1) % count, i) for i in range(count)]),
            ],
            axis=dim,
        )
    return cells


def per_device(kernels, history, incident, owner, tile_pairs, tile_values, tile_counts):
    row_count = lax.axis_size("row")
    col_count = lax.axis_size("col")
    columns = history.shape[2]
    cluster = incident.shape[1]
    retarded = lax.dot_general(
        kernels,
        lax.all_gather(history, "col", axis=1, tiled=True),
        (((0, 2), (0, 1)), ((), ())),
        preferred_element_type=jnp.float32,
    )
    col_index = lax.axis_index("col")
    row_index = lax.axis_index("row")
    block_owner = lax.dynamic_slice_in_dim(owner, col_index * row_count, row_count)
    positions = jnp.arange(row_count, dtype=jnp.int32)
    blocks = retarded.reshape(row_count, cluster, columns)
    block_sum = lax.psum_scatter(blocks, "row", scatter_dimension=0, tiled=True)
    everyone = lax.all_gather(block_sum, "row", axis=0, tiled=True)
    chosen = jnp.sum(jnp.where(block_owner == row_index, positions, 0))
    owned_sum = lax.dynamic_index_in_dim(everyone, chosen, 0, keepdims=False)
    driven = incident[0] - owned_sum
    sources = tile_pairs[:, 1]
    clusters = jnp.arange(owner.shape[0], dtype=jnp.int32)
    src_owner = jnp.sum(jnp.where(sources[:, None] == clusters[None, :], owner[None, :], 0), axis=1)
    src_block = sources // row_count
    window_slot = (src_block - col_index + 1 + col_count) % col_count * row_count + src_owner
    active = jnp.arange(tile_values.shape[0], dtype=jnp.int32) < tile_counts[0]
    density = driven
    for sweep_step in range(SWEEPS):
        rounded = density.astype(jnp.bfloat16)
        block_part = lax.all_gather(rounded, "row", axis=0, tiled=True)
        window = with_halo(block_part, (("col", 0),), row_count * cluster)
        window = window.reshape(-1, cluster, columns)
        picked = jnp.take(window, window_slot, axis=0)
        picked = jnp.where(active[:, None, None], picked, jnp.zeros((), jnp.bfloat16))
        near_term = lax.dot_general(
            tile_values, picked, (((0, 2), (0, 1)), ((), ())), preferred_element_type=jnp.float32
        )
        density = density + damping * (driven - density - near_term)
    return density[None]


def solution(mesh):
    in_specs = (
        P(None, "col", "row"),
        P(None, ("row", "col"), None),
        P(("row", "col"), None, None),
        P(),
        P(("row", "col"), None),
        P(("row", "col"), None, None),
        P(("row", "col")),
    )
    out_specs = P(("row", "col"), None, None)
    return jax.shard_map(
        per_device, mesh=mesh, in_specs=in_specs, out_specs=out_specs, check_vma=False
    )
```

profile of v0, /device:TPU:0, one launch (start us, length us, event | category | flops | bytes accessed | tf_op | source)
XLA Modules:
  0.0 202.0 jit_solution(14236669765198058881)
XLA Ops:
  6.5 0.7 all-gather.2.cloned.1.call-update
  7.3 84.3 %all-gather.2.cloned.1.call-done = bf16[6,1536,256]{2,1,0:T(8,128)(2,1)} async-done(((bf16[6,192,256]{2,1,0:T(8,128)(2,1)}), bf16[6,1536,256]{2,1,0:T(8,128)(2,1)}) %all-gather.2.cloned.1.call-update) | async-done | bytes 4718608 | tf_op jit(solution)/shard_map/all_gather | solution.py:33
  91.6 8.4 %fusion.34 = f32[512,256,1]{1,0,2:T(8,128)} fusion(bf16[6,512,1536]{2,1,0:T(8,128)(2,1)} %param.9, bf16[6,1536,256]{2,1,0:T(8,128)(2,1)} %all-gather.2.cloned.1.call-done), kind=kOutput, calls=%fused_computation.66 | convolution fusion | flops 2415919104 | bytes 14680064 | tf_op jit(solution)/shard_map/dot_general | solution.py:31
  100.1 0.7 fusion.22
  103.7 16.5 %reduce-scatter.2.cloned.1.call-done = f32[1,128,256]{2,1,0:T(8,128)} async-done(((f32[4,128,256]{2,1,0:T(8,128)}), f32[1,128,256]{2,1,0:T(8,128)}) %reduce-scatter.2.cloned.1.call-update) | async-done | bytes 131088 | tf_op jit(solution)/shard_map/reduce_scatter | solution.py:42
  120.2 6.8 %all_gather.16 = f32[4,128,256]{2,1,0:T(8,128)S(1)} all-gather(f32[1,128,256]{2,1,0:T(8,128)} %reduce-scatter.2.cloned.1.call-done), channel_id=1, replica_groups=mesh['row'=4,'col'=8] {'row'}, dimensions={0}, use_global_device_ids=true | all-gather | bytes 655360 | tf_op jit(solution)/shard_map/all_gather | solution.py:43
  127.2 5.9 %all_gather.17 = bf16[512,256]{0,1:T(8,128)(2,1)S(1)} all-gather(bf16[128,256]{0,1:T(8,128)(2,1)S(1)} %get-tuple-element.8), channel_id=1, replica_groups=mesh['row'=4,'col'=8] {'row'}, dimensions={0}, use_global_device_ids=true | all-gather | bytes 327680 | tf_op jit(solution)/shard_map/all_gather | solution.py:56
  133.1 1.5 collective-permute-start
  134.6 3.2 %collective-permute-start.1 = (bf16[512,256]{0,1:T(8,128)(2,1)S(1)}, bf16[512,256]{0,1:T(8,128)(2,1)S(1)}, u32[]{:S(2)}, u32[]{:S(2)}) collective-permute-start(bf16[512,256]{0,1:T(8,128)(2,1)S(1)} %all_gather.17), channel_id=1, source_target_pairs={{1,0},{2,1},{3,2},{4,3},{5,4},{6,5},{7,6},{0,7},{9,8},{10,9},{11,1... | collective-permute-start | bytes 786440 | tf_op jit(solution)/shard_map/ppermute | solution.py:19
  137.8 8.4 %collective-permute-done = bf16[512,256]{0,1:T(8,128)(2,1)S(1)} collective-permute-done((bf16[512,256]{0,1:T(8,128)(2,1)S(1)}, bf16[512,256]{0,1:T(8,128)(2,1)S(1)}, u32[]{:S(2)}, u32[]{:S(2)}) %collective-permute-start) | collective-permute-done | bytes 262176 | tf_op jit(solution)/shard_map/ppermute | solution.py:17
  146.2 2.2 %collective-permute-done.1 = bf16[512,256]{0,1:T(8,128)(2,1)S(1)} collective-permute-done((bf16[512,256]{0,1:T(8,128)(2,1)S(1)}, bf16[512,256]{0,1:T(8,128)(2,1)S(1)}, u32[]{:S(2)}, u32[]{:S(2)}) %collective-permute-start.1) | collective-permute-done | bytes 262176 | tf_op jit(solution)/shard_map/ppermute | solution.py:19
  148.8 0.6 gather_fusion
  149.4 0.5 fusion.32
  149.9 5.8 %all_gather.18 = bf16[512,256]{0,1:T(8,128)(2,1)S(1)} all-gather(bf16[128,256]{0,1:T(8,128)(2,1)S(1)} %get-tuple-element.10), channel_id=1, replica_groups=mesh['row'=4,'col'=8] {'row'}, dimensions={0}, use_global_device_ids=true | all-gather | bytes 327680 | tf_op jit(solution)/shard_map/all_gather | solution.py:56
  156.0 4.4 %collective-permute-start.3 = (bf16[512,256]{0,1:T(8,128)(2,1)S(1)}, bf16[512,256]{0,1:T(8,128)(2,1)S(1)}, u32[]{:S(2)}, u32[]{:S(2)}) collective-permute-start(bf16[512,256]{0,1:T(8,128)(2,1)S(1)} %all_gather.18), channel_id=1, source_target_pairs={{1,0},{2,1},{3,2},{4,3},{5,4},{6,5},{7,6},{0,7},{9,8},{10,9},{11,1... | collective-permute-start | bytes 786440 | tf_op jit(solution)/shard_map/ppermute | solution.py:19
  160.5 7.3 %collective-permute-done.2 = bf16[512,256]{0,1:T(8,128)(2,1)S(1)} collective-permute-done((bf16[512,256]{0,1:T(8,128)(2,1)S(1)}, bf16[512,256]{0,1:T(8,128)(2,1)S(1)}, u32[]{:S(2)}, u32[]{:S(2)}) %collective-permute-start.2) | collective-permute-done | bytes 262176 | tf_op jit(solution)/shard_map/ppermute | solution.py:17
  167.7 2.8 %collective-permute-done.3 = bf16[512,256]{0,1:T(8,128)(2,1)S(1)} collective-permute-done((bf16[512,256]{0,1:T(8,128)(2,1)S(1)}, bf16[512,256]{0,1:T(8,128)(2,1)S(1)}, u32[]{:S(2)}, u32[]{:S(2)}) %collective-permute-start.3) | collective-permute-done | bytes 262176 | tf_op jit(solution)/shard_map/ppermute | solution.py:19
  170.9 0.6 gather_fusion.1
  172.0 5.8 %all_gather.19 = bf16[512,256]{0,1:T(8,128)(2,1)S(1)} all-gather(bf16[128,256]{0,1:T(8,128)(2,1)S(1)} %get-tuple-element.12), channel_id=1, replica_groups=mesh['row'=4,'col'=8] {'row'}, dimensions={0}, use_global_device_ids=true | all-gather | bytes 327680 | tf_op jit(solution)/shard_map/all_gather | solution.py:56
  177.8 4.7 %collective-permute-start.5 = (bf16[512,256]{0,1:T(8,128)(2,1)S(1)}, bf16[512,256]{0,1:T(8,128)(2,1)S(1)}, u32[]{:S(2)}, u32[]{:S(2)}) collective-permute-start(bf16[512,256]{0,1:T(8,128)(2,1)S(1)} %all_gather.19), channel_id=1, source_target_pairs={{1,0},{2,1},{3,2},{4,3},{5,4},{6,5},{7,6},{0,7},{9,8},{10,9},{11,1... | collective-permute-start | bytes 786440 | tf_op jit(solution)/shard_map/ppermute | solution.py:19
  182.5 7.3 %collective-permute-done.4 = bf16[512,256]{0,1:T(8,128)(2,1)S(1)} collective-permute-done((bf16[512,256]{0,1:T(8,128)(2,1)S(1)}, bf16[512,256]{0,1:T(8,128)(2,1)S(1)}, u32[]{:S(2)}, u32[]{:S(2)}) %collective-permute-start.4) | collective-permute-done | bytes 262176 | tf_op jit(solution)/shard_map/ppermute | solution.py:17
  189.8 3.1 %collective-permute-done.5 = bf16[512,256]{0,1:T(8,128)(2,1)S(1)} collective-permute-done((bf16[512,256]{0,1:T(8,128)(2,1)S(1)}, bf16[512,256]{0,1:T(8,128)(2,1)S(1)}, u32[]{:S(2)}, u32[]{:S(2)}) %collective-permute-start.5) | collective-permute-done | bytes 262176 | tf_op jit(solution)/shard_map/ppermute | solution.py:19
  193.2 0.6 gather_fusion.2
  194.4 0.8 copy.37
  (29 shorter events, 2.8 us)
Async XLA Ops:
  6.5 142.9 %copy-start = (bf16[12,128,128]{2,1,0:T(8,128)(2,1)S(1)}, bf16[12,128,128]{2,1,0:T(8,128)(2,1)}, u32[]{:S(2)}) copy-start(bf16[12,128,128]{2,1,0:T(8,128)(2,1)} %param.14) | copy-start | bytes 1179652
  6.5 85.1 %all-gather.2.cloned.1.call-start = ((), (), s32[]{:S(2)}) async-start(), calls=%async_computation.1 | async-start | bytes 5308416 | tf_op jit(solution)/shard_map/all_gather | solution.py:33
  7.3 92.8 %copy-start.2 = (s32[32]{0:T(128)S(1)}, s32[32]{0:T(128)}, u32[]{:S(2)}) copy-start(s32[32]{0:T(128)} %param.12) | copy-start | bytes 388
  7.3 94.8 %copy-start.1 = (f32[1,128,256]{2,1,0:T(8,128)S(1)}, f32[1,128,256]{2,1,0:T(8,128)}, u32[]{:S(2)}) copy-start(f32[1,128,256]{2,1,0:T(8,128)} %param.11) | copy-start | bytes 393220
  7.3 96.2 %copy-start.3 = (s32[12,2]{0,1:T(2,128)S(1)}, s32[12,2]{0,1:T(2,128)}, u32[]{:S(2)}) copy-start(s32[12,2]{0,1:T(2,128)} %param.13) | copy-start | bytes 292
  7.3 112.9 %reduce-scatter.2.cloned.1.call-start = ((), (), s32[]{:S(2)}) async-start(), calls=%async_computation.2 | async-start | bytes 655360 | tf_op jit(solution)/shard_map/reduce_scatter | solution.py:42
  133.1 13.2 %collective-permute-start = (bf16[512,256]{0,1:T(8,128)(2,1)S(1)}, bf16[512,256]{0,1:T(8,128)(2,1)S(1)}, u32[]{:S(2)}, u32[]{:S(2)}) collective-permute-start(bf16[512,256]{0,1:T(8,128)(2,1)S(1)} %all_gather.17), channel_id=1, source_target_pairs={{0,1},{1,2},{2,3},{3,4},{4,5},{5,6},{6,7},{7,0},{8,9},{9,10},{10,1... | collective-permute-start | bytes 786440 | tf_op jit(solution)/shard_map/ppermute | solution.py:17
  134.6 13.9 %collective-permute-start.1 = (bf16[512,256]{0,1:T(8,128)(2,1)S(1)}, bf16[512,256]{0,1:T(8,128)(2,1)S(1)}, u32[]{:S(2)}, u32[]{:S(2)}) collective-permute-start(bf16[512,256]{0,1:T(8,128)(2,1)S(1)} %all_gather.17), channel_id=1, source_target_pairs={{1,0},{2,1},{3,2},{4,3},{5,4},{6,5},{7,6},{0,7},{9,8},{10,9},{11,1... | collective-permute-start | bytes 786440 | tf_op jit(solution)/shard_map/ppermute | solution.py:19
  155.7 12.0 %collective-permute-start.2 = (bf16[512,256]{0,1:T(8,128)(2,1)S(1)}, bf16[512,256]{0,1:T(8,128)(2,1)S(1)}, u32[]{:S(2)}, u32[]{:S(2)}) collective-permute-start(bf16[512,256]{0,1:T(8,128)(2,1)S(1)} %all_gather.18), channel_id=1, source_target_pairs={{0,1},{1,2},{2,3},{3,4},{4,5},{5,6},{6,7},{7,0},{8,9},{9,10},{10,1... | collective-permute-start | bytes 786440 | tf_op jit(solution)/shard_map/ppermute | solution.py:17
  156.0 14.5 %collective-permute-start.3 = (bf16[512,256]{0,1:T(8,128)(2,1)S(1)}, bf16[512,256]{0,1:T(8,128)(2,1)S(1)}, u32[]{:S(2)}, u32[]{:S(2)}) collective-permute-start(bf16[512,256]{0,1:T(8,128)(2,1)S(1)} %all_gather.18), channel_id=1, source_target_pairs={{1,0},{2,1},{3,2},{4,3},{5,4},{6,5},{7,6},{0,7},{9,8},{10,9},{11,1... | collective-permute-start | bytes 786440 | tf_op jit(solution)/shard_map/ppermute | solution.py:19
  177.8 12.0 %collective-permute-start.4 = (bf16[512,256]{0,1:T(8,128)(2,1)S(1)}, bf16[512,256]{0,1:T(8,128)(2,1)S(1)}, u32[]{:S(2)}, u32[]{:S(2)}) collective-permute-start(bf16[512,256]{0,1:T(8,128)(2,1)S(1)} %all_gather.19), channel_id=1, source_target_pairs={{0,1},{1,2},{2,3},{3,4},{4,5},{5,6},{6,7},{7,0},{8,9},{9,10},{10,1... | collective-permute-start | bytes 786440 | tf_op jit(solution)/shard_map/ppermute | solution.py:17
  177.8 15.1 %collective-permute-start.5 = (bf16[512,256]{0,1:T(8,128)(2,1)S(1)}, bf16[512,256]{0,1:T(8,128)(2,1)S(1)}, u32[]{:S(2)}, u32[]{:S(2)}) collective-permute-start(bf16[512,256]{0,1:T(8,128)(2,1)S(1)} %all_gather.19), channel_id=1, source_target_pairs={{1,0},{2,1},{3,2},{4,3},{5,4},{6,5},{7,6},{0,7},{9,8},{10,9},{11,1... | collective-permute-start | bytes 786440 | tf_op jit(solution)/shard_map/ppermute | solution.py:19
Sparse Core Ops, SparseCore 0:
  9.5 82.0 all-gather.1
  100.2 20.0 reduce-scatter.1
where the time goes:
time: 202 us
  waiting for transfers between devices  133 us (66%)
  blocking collectives  24.3 us (12%)
  between operations  16.2 us (8%)
  starting transfers between devices  14.2 us (7%)
  matrix products  10 us (5%)
  local copies, waits for them, and re-layouts  3.57 us (2%)
    all_gather x1, waiting for transfers between devices, per_device(): lax.all_gather(history, 'col', axis=1, tiled=True)  84.3 us
    ppermute x3, waiting for transfers between devices, with_halo(): lax.ppermute(tail, axis, [(i, (i + 1) % count) for i in range(count)])  22.9 us
    all_gather x3, blocking collectives, per_device(): block_part = lax.all_gather(rounded, 'row', axis=0, tiled=True)  17.5 us
    reduce_scatter x1, waiting for transfers between devices, per_device(): block_sum = lax.psum_scatter(blocks, 'row', scatter_dimension=0, tiled=True)  16.5 us
    ppermute x3, starting transfers between devices, with_halo(): lax.ppermute(head, axis, [((i + 1) % count, i) for i in range(count)])  12.4 us
    dot_general x1, matrix products, per_device(): lax.dot_general(kernels, lax.all_gather(history, 'col', axis=1, tiled=Tru...  8.41 us
    ppermute x3, waiting for transfers between devices, with_halo(): lax.ppermute(head, axis, [((i + 1) % count, i) for i in range(count)])  8.1 us
    all_gather x1, blocking collectives, per_device(): everyone = lax.all_gather(block_sum, 'row', axis=0, tiled=True)  6.78 us
  transfers between devices with their start and end apart: 8, of which 8 were waited for; matrix products, arithmetic and copies ran while one was open for 1% of the time, Pallas kernels for 0%

commit v1 on v0

--- a/solution.py
+++ b/solution.py
@@ -1,3 +1,4 @@
+import functools
 import jax
 import jax.numpy as jnp
 from jax import lax
@@ -5,6 +6,26 @@
 
 SWEEPS = 3
 damping = 0.7
+
+
+def pass_spots_on_mesh(mat, pos_dim):
+    res = list(mat.shape[1:])
+    res[pos_dim] *= mat.shape[0]
+    return jnp.moveaxis(mat, 0, pos_dim).reshape(res)
+
+
+def _show_limits(z, device_axis, dim_k):
+    n_chips = jax.lax.axis_size(device_axis)
+    crops = list(map(lambda dev_j: (dev_j, (dev_j + 1) % n_chips), range(n_chips)))
+    kept_rows = [z]
+    while len(kept_rows) < n_chips:
+        kept_rows.append(jax.lax.ppermute(kept_rows[-1], axis_name=device_axis, perm=crops))
+    new = jax.lax.axis_index(device_axis)
+    kept_rows = jnp.stack(kept_rows)[(new - jnp.arange(n_chips)) % n_chips]
+    return pass_spots_on_mesh(kept_rows, dim_k)
+
+
+advance_boxes = functools.partial(_show_limits, device_axis="col", dim_k=1)
 
 
 def with_halo(cells, sides, width):
@@ -30,7 +51,7 @@
     cluster = incident.shape[1]
     retarded = lax.dot_general(
         kernels,
-        lax.all_gather(history, "col", axis=1, tiled=True),
+        advance_boxes(history),
         (((0, 2), (0, 1)), ((), ())),
         preferred_element_type=jnp.float32,
     )

time: 202 us -> 231 us (1.14)
  local copies, waits for them, and re-layouts: 3.57 us -> 20.5 us
  waiting for transfers between devices: 133 us -> 147 us
  matrix products: 10 us -> 6.92 us
    ppermute x0 -> x7, waiting for transfers between devices: none -> 99.7 us  [_show_limits(): jax.lax.ppermute(kept_rows[-1], axis_name=device_axis, perm=crops)]
    all_gather x1 -> x0, waiting for transfers between devices: 84.3 us -> none  [per_device(): lax.all_gather(history, 'col', axis=1, tiled=True)]
    ppermute x3, waiting for transfers between devices: 8.1 us -> 23.3 us  [with_halo(): lax.ppermute(head, axis, [((i + 1) % count, i) for i in range(count)])]
    ppermute x3, waiting for transfers between devices: 22.9 us -> 9.98 us  [with_halo(): lax.ppermute(tail, axis, [(i, (i + 1) % count) for i in range(count)])]
    unnamed x10 -> x17, local copies, waits for them, and re-layouts: 0.19 us -> 7.29 us
    gather x0 -> x1, local copies, waits for them, and re-layouts: none -> 5.36 us  [_show_limits(): kept_rows = jnp.stack(kept_rows)[(new - jnp.arange(n_chips)) % n_chips]]
    dot_general x1, matrix products: 8.41 us -> 5.31 us  [per_device(): lax.dot_general(kernels, advance_boxes(history), (((0, 2), (0, 1)), ((),...]
    ppermute x0 -> x7, starting transfers between devices: none -> 2.98 us  [_show_limits(): jax.lax.ppermute(kept_rows[-1], axis_name=device_axis, perm=crops)]
  transfers between devices with their start and end apart: 8 -> 14, of which waited for: 8 -> 14; matrix products, arithmetic and copies ran while one was open for 1% -> 4% of each run, Pallas kernels for 0% -> 0%
where the time goes in v1:
time: 231 us; the launch traced here: 230 us
  waiting for transfers between devices  147 us (64%)
  blocking collectives  24.3 us (11%)
  local copies, waits for them, and re-layouts  20.5 us (9%)
  between operations  16.2 us (7%)
  starting transfers between devices  13.9 us (6%)
  matrix products  6.92 us (3%)
    ppermute x7, waiting for transfers between devices, _show_limits(): jax.lax.ppermute(kept_rows[-1], axis_name=device_axis, perm=crops)  99.7 us
    ppermute x3, waiting for transfers between devices, with_halo(): lax.ppermute(head, axis, [((i + 1) % count, i) for i in range(count)])  23.3 us
    all_gather x3, blocking collectives, per_device(): block_part = lax.all_gather(rounded, 'row', axis=0, tiled=True)  17.5 us
    reduce_scatter x1, waiting for transfers between devices, per_device(): block_sum = lax.psum_scatter(blocks, 'row', scatter_dimension=0, tiled=True)  14.3 us
    ppermute x3, starting transfers between devices, with_halo(): lax.ppermute(head, axis, [((i + 1) % count, i) for i in range(count)])  10.9 us
    ppermute x3, waiting for transfers between devices, with_halo(): lax.ppermute(tail, axis, [(i, (i + 1) % count) for i in range(count)])  9.98 us
    unnamed x17, local copies, waits for them, and re-layouts  7.29 us
    all_gather x1, blocking collectives, per_device(): everyone = lax.all_gather(block_sum, 'row', axis=0, tiled=True)  6.8 us
  transfers between devices with their start and end apart: 14, of which 14 were waited for; matrix products, arithmetic and copies ran while one was open for 4% of the time, Pallas kernels for 0%

profile of v1, /device:TPU:0, one launch (start us, length us, event | category | flops | bytes accessed | tf_op | source)
XLA Modules:
  0.0 230.3 jit_solution(4243331254793581546)
XLA Ops:
  6.5 3.0 %collective-permute-start = (bf16[6,192,256]{2,1,0:T(8,128)(2,1)}, bf16[6,192,256]{2,1,0:T(8,128)(2,1)S(1)}, u32[]{:S(2)}, u32[]{:S(2)}) collective-permute-start(bf16[6,192,256]{2,1,0:T(8,128)(2,1)} %param.10), channel_id=1, source_target_pairs={{0,1},{1,2},{2,3},{3,4},{4,5},{5,6},{6,7},{7,0},{8,9},{9,10},{10,1... | collective-permute-start | bytes 1769480 | tf_op jit(solution)/shard_map/ppermute | solution.py:22
  9.5 16.6 %collective-permute-done = bf16[6,192,256]{2,1,0:T(8,128)(2,1)S(1)} collective-permute-done((bf16[6,192,256]{2,1,0:T(8,128)(2,1)}, bf16[6,192,256]{2,1,0:T(8,128)(2,1)S(1)}, u32[]{:S(2)}, u32[]{:S(2)}) %collective-permute-start) | collective-permute-done | bytes 589856 | tf_op jit(solution)/shard_map/ppermute | solution.py:22
  26.1 17.2 %collective-permute-done.1 = bf16[6,192,256]{2,1,0:T(8,128)(2,1)S(1)} collective-permute-done((bf16[6,192,256]{2,1,0:T(8,128)(2,1)S(1)}, bf16[6,192,256]{2,1,0:T(8,128)(2,1)S(1)}, u32[]{:S(2)}, u32[]{:S(2)}) %collective-permute-start.1) | collective-permute-done | bytes 589856 | tf_op jit(solution)/shard_map/ppermute | solution.py:22
  43.3 16.3 %collective-permute-done.2 = bf16[6,192,256]{2,1,0:T(8,128)(2,1)S(1)} collective-permute-done((bf16[6,192,256]{2,1,0:T(8,128)(2,1)S(1)}, bf16[6,192,256]{2,1,0:T(8,128)(2,1)S(1)}, u32[]{:S(2)}, u32[]{:S(2)}) %collective-permute-start.2) | collective-permute-done | bytes 589856 | tf_op jit(solution)/shard_map/ppermute | solution.py:22
  59.6 15.5 %collective-permute-done.3 = bf16[6,192,256]{2,1,0:T(8,128)(2,1)S(1)} collective-permute-done((bf16[6,192,256]{2,1,0:T(8,128)(2,1)S(1)}, bf16[6,192,256]{2,1,0:T(8,128)(2,1)S(1)}, u32[]{:S(2)}, u32[]{:S(2)}) %collective-permute-start.3) | collective-permute-done | bytes 589856 | tf_op jit(solution)/shard_map/ppermute | solution.py:22
  77.0 12.7 %collective-permute-done.4 = bf16[6,192,256]{2,1,0:T(8,128)(2,1)S(1)} collective-permute-done((bf16[6,192,256]{2,1,0:T(8,128)(2,1)S(1)}, bf16[6,192,256]{2,1,0:T(8,128)(2,1)S(1)}, u32[]{:S(2)}, u32[]{:S(2)}) %collective-permute-start.4) | collective-permute-done | bytes 589856 | tf_op jit(solution)/shard_map/ppermute | solution.py:22
  92.3 11.2 %collective-permute-done.5 = bf16[6,192,256]{2,1,0:T(8,128)(2,1)S(1)} collective-permute-done((bf16[6,192,256]{2,1,0:T(8,128)(2,1)S(1)}, bf16[6,192,256]{2,1,0:T(8,128)(2,1)S(1)}, u32[]{:S(2)}, u32[]{:S(2)}) %collective-permute-start.5) | collective-permute-done | bytes 589856 | tf_op jit(solution)/shard_map/ppermute | solution.py:22
  106.0 10.3 %collective-permute-done.6 = bf16[6,192,256]{2,1,0:T(8,128)(2,1)S(1)} collective-permute-done((bf16[6,192,256]{2,1,0:T(8,128)(2,1)S(1)}, bf16[6,192,256]{2,1,0:T(8,128)(2,1)S(1)}, u32[]{:S(2)}, u32[]{:S(2)}) %collective-permute-start.6) | collective-permute-done | bytes 589856 | tf_op jit(solution)/shard_map/ppermute | solution.py:22
  117.2 5.4 %gather_fusion = bf16[8,6,192,256]{3,2,1,0:T(8,128)(2,1)} fusion(bf16[8,6,192,256]{3,2,1,0:T(8,128)(2,1)} %bitcast_dynamic-update-slice_fusion, s32[1024]{0:T(1024)S(1)} %pad_clamp_fusion.1), kind=kCustom, calls=%fused_computation.3 | custom fusion | bytes 9437216 | tf_op jit(solution)/shard_map/gather | solution.py:24
  122.6 2.6 %copy.44 = bf16[6,8,192,256]{3,2,1,0:T(8,128)(2,1)S(1)} copy(bf16[6,8,192,256]{3,2,0,1:T(8,128)(2,1)} %bitcast.86) | data formatting | bytes 9437184 | tf_op jit(solution)/shard_map/transpose | solution.py:14
  125.3 5.3 %convolution_bitcast_fusion = f32[512,256]{0,1:T(8,128)S(1)} fusion(bf16[6,1536,256]{2,1,0:T(8,128)(2,1)S(1)} %bitcast.87, bf16[6,512,1536]{2,1,0:T(8,128)(2,1)} %param.9), kind=kOutput, calls=%fused_computation.4 | convolution fusion | flops 2415919104 | bytes 14680064 | tf_op jit(solution)/shard_map/dot_general | solution.py:52
  135.3 14.3 %reduce-scatter.2.cloned.1.call-done = f32[1,128,256]{2,1,0:T(8,128)} async-done(((f32[4,128,256]{2,1,0:T(8,128)}), f32[1,128,256]{2,1,0:T(8,128)}) %reduce-scatter.2.cloned.1.call-update) | async-done | bytes 131088 | tf_op jit(solution)/shard_map/reduce_scatter | solution.py:63
  149.6 6.8 %all_gather.12 = f32[4,128,256]{2,1,0:T(8,128)S(1)} all-gather(f32[1,128,256]{2,1,0:T(8,128)} %reduce-scatter.2.cloned.1.call-done), channel_id=1, replica_groups=mesh['row'=4,'col'=8] {'row'}, dimensions={0}, use_global_device_ids=true | all-gather | bytes 655360 | tf_op jit(solution)/shard_map/all_gather | solution.py:64
  156.5 5.9 %all_gather.13 = bf16[512,256]{0,1:T(8,128)(2,1)S(1)} all-gather(bf16[128,256]{0,1:T(8,128)(2,1)S(1)} %get-tuple-element.8), channel_id=1, replica_groups=mesh['row'=4,'col'=8] {'row'}, dimensions={0}, use_global_device_ids=true | all-gather | bytes 327680 | tf_op jit(solution)/shard_map/all_gather | solution.py:77
  162.4 4.2 %collective-permute-start.8 = (bf16[512,256]{0,1:T(8,128)(2,1)S(1)}, bf16[512,256]{0,1:T(8,128)(2,1)S(1)}, u32[]{:S(2)}, u32[]{:S(2)}) collective-permute-start(bf16[512,256]{0,1:T(8,128)(2,1)S(1)} %all_gather.13), channel_id=1, source_target_pairs={{1,0},{2,1},{3,2},{4,3},{5,4},{6,5},{7,6},{0,7},{9,8},{10,9},{11,1... | collective-permute-start | bytes 786440 | tf_op jit(solution)/shard_map/ppermute | solution.py:40
  166.7 6.0 %collective-permute-done.8 = bf16[512,256]{0,1:T(8,128)(2,1)S(1)} collective-permute-done((bf16[512,256]{0,1:T(8,128)(2,1)S(1)}, bf16[512,256]{0,1:T(8,128)(2,1)S(1)}, u32[]{:S(2)}, u32[]{:S(2)}) %collective-permute-start.8) | collective-permute-done | bytes 262176 | tf_op jit(solution)/shard_map/ppermute | solution.py:40
  172.7 4.9 %collective-permute-done.7 = bf16[512,256]{0,1:T(8,128)(2,1)S(1)} collective-permute-done((bf16[512,256]{0,1:T(8,128)(2,1)S(1)}, bf16[512,256]{0,1:T(8,128)(2,1)S(1)}, u32[]{:S(2)}, u32[]{:S(2)}) %collective-permute-start.7) | collective-permute-done | bytes 262176 | tf_op jit(solution)/shard_map/ppermute | solution.py:38
  179.1 5.8 %all_gather.14 = bf16[512,256]{0,1:T(8,128)(2,1)S(1)} all-gather(bf16[128,256]{0,1:T(8,128)(2,1)S(1)} %get-tuple-element.10), channel_id=1, replica_groups=mesh['row'=4,'col'=8] {'row'}, dimensions={0}, use_global_device_ids=true | all-gather | bytes 327680 | tf_op jit(solution)/shard_map/all_gather | solution.py:77
  184.9 3.5 %collective-permute-start.10 = (bf16[512,256]{0,1:T(8,128)(2,1)S(1)}, bf16[512,256]{0,1:T(8,128)(2,1)S(1)}, u32[]{:S(2)}, u32[]{:S(2)}) collective-permute-start(bf16[512,256]{0,1:T(8,128)(2,1)S(1)} %all_gather.14), channel_id=1, source_target_pairs={{1,0},{2,1},{3,2},{4,3},{5,4},{6,5},{7,6},{0,7},{9,8},{10,9},{11,1... | collective-permute-start | bytes 786440 | tf_op jit(solution)/shard_map/ppermute | solution.py:40
  188.4 6.1 %collective-permute-done.10 = bf16[512,256]{0,1:T(8,128)(2,1)S(1)} collective-permute-done((bf16[512,256]{0,1:T(8,128)(2,1)S(1)}, bf16[512,256]{0,1:T(8,128)(2,1)S(1)}, u32[]{:S(2)}, u32[]{:S(2)}) %collective-permute-start.10) | collective-permute-done | bytes 262176 | tf_op jit(solution)/shard_map/ppermute | solution.py:40
  194.5 4.9 %collective-permute-done.9 = bf16[512,256]{0,1:T(8,128)(2,1)S(1)} collective-permute-done((bf16[512,256]{0,1:T(8,128)(2,1)S(1)}, bf16[512,256]{0,1:T(8,128)(2,1)S(1)}, u32[]{:S(2)}, u32[]{:S(2)}) %collective-permute-start.9) | collective-permute-done | bytes 262176 | tf_op jit(solution)/shard_map/ppermute | solution.py:38
  200.8 5.8 %all_gather.15 = bf16[512,256]{0,1:T(8,128)(2,1)S(1)} all-gather(bf16[128,256]{0,1:T(8,128)(2,1)S(1)} %get-tuple-element.12), channel_id=1, replica_groups=mesh['row'=4,'col'=8] {'row'}, dimensions={0}, use_global_device_ids=true | all-gather | bytes 327680 | tf_op jit(solution)/shard_map/all_gather | solution.py:77
  206.7 3.2 %collective-permute-start.12 = (bf16[512,256]{0,1:T(8,128)(2,1)S(1)}, bf16[512,256]{0,1:T(8,128)(2,1)S(1)}, u32[]{:S(2)}, u32[]{:S(2)}) collective-permute-start(bf16[512,256]{0,1:T(8,128)(2,1)S(1)} %all_gather.15), channel_id=1, source_target_pairs={{1,0},{2,1},{3,2},{4,3},{5,4},{6,5},{7,6},{0,7},{9,8},{10,9},{11,1... | collective-permute-start | bytes 786440 | tf_op jit(solution)/shard_map/ppermute | solution.py:40
  209.9 11.2 %collective-permute-done.12 = bf16[512,256]{0,1:T(8,128)(2,1)S(1)} collective-permute-done((bf16[512,256]{0,1:T(8,128)(2,1)S(1)}, bf16[512,256]{0,1:T(8,128)(2,1)S(1)}, u32[]{:S(2)}, u32[]{:S(2)}) %collective-permute-start.12) | collective-permute-done | bytes 262176 | tf_op jit(solution)/shard_map/ppermute | solution.py:40
  (53 shorter events, 15.5 us)
Async XLA Ops:
  6.5 172.0 %copy-start = (bf16[12,128,128]{2,1,0:T(8,128)(2,1)S(1)}, bf16[12,128,128]{2,1,0:T(8,128)(2,1)}, u32[]{:S(2)}) copy-start(bf16[12,128,128]{2,1,0:T(8,128)(2,1)} %param.14) | copy-start | bytes 1179652
  6.5 143.0 %reduce-scatter.2.cloned.1.call-start = ((), (), s32[]{:S(2)}) async-start(), calls=%async_computation.1 | async-start | bytes 655360 | tf_op jit(solution)/shard_map/reduce_scatter | solution.py:63
  6.5 19.5 %collective-permute-start = (bf16[6,192,256]{2,1,0:T(8,128)(2,1)}, bf16[6,192,256]{2,1,0:T(8,128)(2,1)S(1)}, u32[]{:S(2)}, u32[]{:S(2)}) collective-permute-start(bf16[6,192,256]{2,1,0:T(8,128)(2,1)} %param.10), channel_id=1, source_target_pairs={{0,1},{1,2},{2,3},{3,4},{4,5},{5,6},{6,7},{7,0},{8,9},{9,10},{10,1... | collective-permute-start | bytes 1769480 | tf_op jit(solution)/shard_map/ppermute | solution.py:22
  26.1 17.2 %collective-permute-start.1 = (bf16[6,192,256]{2,1,0:T(8,128)(2,1)S(1)}, bf16[6,192,256]{2,1,0:T(8,128)(2,1)S(1)}, u32[]{:S(2)}, u32[]{:S(2)}) collective-permute-start(bf16[6,192,256]{2,1,0:T(8,128)(2,1)S(1)} %collective-permute-done), channel_id=1, source_target_pairs={{0,1},{1,2},{2,3},{3,4},{4,5},{5,6},{6,7},{7,0},{8,9},{9,10},{10,1... | collective-permute-start | bytes 1769480 | tf_op jit(solution)/shard_map/ppermute | solution.py:22
  43.3 16.3 %collective-permute-start.2 = (bf16[6,192,256]{2,1,0:T(8,128)(2,1)S(1)}, bf16[6,192,256]{2,1,0:T(8,128)(2,1)S(1)}, u32[]{:S(2)}, u32[]{:S(2)}) collective-permute-start(bf16[6,192,256]{2,1,0:T(8,128)(2,1)S(1)} %collective-permute-done.1), channel_id=1, source_target_pairs={{0,1},{1,2},{2,3},{3,4},{4,5},{5,6},{6,7},{7,0},{8,9},{9,10},{10,1... | collective-permute-start | bytes 1769480 | tf_op jit(solution)/shard_map/ppermute | solution.py:22
  59.6 15.5 %collective-permute-start.3 = (bf16[6,192,256]{2,1,0:T(8,128)(2,1)S(1)}, bf16[6,192,256]{2,1,0:T(8,128)(2,1)S(1)}, u32[]{:S(2)}, u32[]{:S(2)}) collective-permute-start(bf16[6,192,256]{2,1,0:T(8,128)(2,1)S(1)} %collective-permute-done.2), channel_id=1, source_target_pairs={{0,1},{1,2},{2,3},{3,4},{4,5},{5,6},{6,7},{7,0},{8,9},{9,10},{10,1... | collective-permute-start | bytes 1769480 | tf_op jit(solution)/shard_map/ppermute | solution.py:22
  75.1 14.6 %collective-permute-start.4 = (bf16[6,192,256]{2,1,0:T(8,128)(2,1)S(1)}, bf16[6,192,256]{2,1,0:T(8,128)(2,1)S(1)}, u32[]{:S(2)}, u32[]{:S(2)}) collective-permute-start(bf16[6,192,256]{2,1,0:T(8,128)(2,1)S(1)} %collective-permute-done.3), channel_id=1, source_target_pairs={{0,1},{1,2},{2,3},{3,4},{4,5},{5,6},{6,7},{7,0},{8,9},{9,10},{10,1... | collective-permute-start | bytes 1769480 | tf_op jit(solution)/shard_map/ppermute | solution.py:22
  89.7 13.8 %collective-permute-start.5 = (bf16[6,192,256]{2,1,0:T(8,128)(2,1)S(1)}, bf16[6,192,256]{2,1,0:T(8,128)(2,1)S(1)}, u32[]{:S(2)}, u32[]{:S(2)}) collective-permute-start(bf16[6,192,256]{2,1,0:T(8,128)(2,1)S(1)} %collective-permute-done.4), channel_id=1, source_target_pairs={{0,1},{1,2},{2,3},{3,4},{4,5},{5,6},{6,7},{7,0},{8,9},{9,10},{10,1... | collective-permute-start | bytes 1769480 | tf_op jit(solution)/shard_map/ppermute | solution.py:22
  103.5 12.9 %collective-permute-start.6 = (bf16[6,192,256]{2,1,0:T(8,128)(2,1)S(1)}, bf16[6,192,256]{2,1,0:T(8,128)(2,1)S(1)}, u32[]{:S(2)}, u32[]{:S(2)}) collective-permute-start(bf16[6,192,256]{2,1,0:T(8,128)(2,1)S(1)} %collective-permute-done.5), channel_id=1, source_target_pairs={{0,1},{1,2},{2,3},{3,4},{4,5},{5,6},{6,7},{7,0},{8,9},{9,10},{10,1... | collective-permute-start | bytes 1769480 | tf_op jit(solution)/shard_map/ppermute | solution.py:22
  125.3 6.4 %copy-start.2 = (s32[32]{0:T(128)S(1)}, s32[32]{0:T(128)}, u32[]{:S(2)}) copy-start(s32[32]{0:T(128)} %param.12) | copy-start | bytes 388
  125.3 8.4 %copy-start.1 = (f32[1,128,256]{2,1,0:T(8,128)S(1)}, f32[1,128,256]{2,1,0:T(8,128)}, u32[]{:S(2)}) copy-start(f32[1,128,256]{2,1,0:T(8,128)} %param.11) | copy-start | bytes 393220
  125.3 9.8 %copy-start.3 = (s32[12,2]{0,1:T(2,128)S(1)}, s32[12,2]{0,1:T(2,128)}, u32[]{:S(2)}) copy-start(s32[12,2]{0,1:T(2,128)} %param.13) | copy-start | bytes 292
  162.4 10.3 %collective-permute-start.8 = (bf16[512,256]{0,1:T(8,128)(2,1)S(1)}, bf16[512,256]{0,1:T(8,128)(2,1)S(1)}, u32[]{:S(2)}, u32[]{:S(2)}) collective-permute-start(bf16[512,256]{0,1:T(8,128)(2,1)S(1)} %all_gather.13), channel_id=1, source_target_pairs={{1,0},{2,1},{3,2},{4,3},{5,4},{6,5},{7,6},{0,7},{9,8},{10,9},{11,1... | collective-permute-start | bytes 786440 | tf_op jit(solution)/shard_map/ppermute | solution.py:40
  166.7 11.0 %collective-permute-start.7 = (bf16[512,256]{0,1:T(8,128)(2,1)S(1)}, bf16[512,256]{0,1:T(8,128)(2,1)S(1)}, u32[]{:S(2)}, u32[]{:S(2)}) collective-permute-start(bf16[512,256]{0,1:T(8,128)(2,1)S(1)} %all_gather.13), channel_id=1, source_target_pairs={{0,1},{1,2},{2,3},{3,4},{4,5},{5,6},{6,7},{7,0},{8,9},{9,10},{10,1... | collective-permute-start | bytes 786440 | tf_op jit(solution)/shard_map/ppermute | solution.py:38
  184.9 9.5 %collective-permute-start.10 = (bf16[512,256]{0,1:T(8,128)(2,1)S(1)}, bf16[512,256]{0,1:T(8,128)(2,1)S(1)}, u32[]{:S(2)}, u32[]{:S(2)}) collective-permute-start(bf16[512,256]{0,1:T(8,128)(2,1)S(1)} %all_gather.14), channel_id=1, source_target_pairs={{1,0},{2,1},{3,2},{4,3},{5,4},{6,5},{7,6},{0,7},{9,8},{10,9},{11,1... | collective-permute-start | bytes 786440 | tf_op jit(solution)/shard_map/ppermute | solution.py:40
  188.4 11.0 %collective-permute-start.9 = (bf16[512,256]{0,1:T(8,128)(2,1)S(1)}, bf16[512,256]{0,1:T(8,128)(2,1)S(1)}, u32[]{:S(2)}, u32[]{:S(2)}) collective-permute-start(bf16[512,256]{0,1:T(8,128)(2,1)S(1)} %all_gather.14), channel_id=1, source_target_pairs={{0,1},{1,2},{2,3},{3,4},{4,5},{5,6},{6,7},{7,0},{8,9},{9,10},{10,1... | collective-permute-start | bytes 786440 | tf_op jit(solution)/shard_map/ppermute | solution.py:38
  206.7 14.4 %collective-permute-start.12 = (bf16[512,256]{0,1:T(8,128)(2,1)S(1)}, bf16[512,256]{0,1:T(8,128)(2,1)S(1)}, u32[]{:S(2)}, u32[]{:S(2)}) collective-permute-start(bf16[512,256]{0,1:T(8,128)(2,1)S(1)} %all_gather.15), channel_id=1, source_target_pairs={{1,0},{2,1},{3,2},{4,3},{5,4},{6,5},{7,6},{0,7},{9,8},{10,9},{11,1... | collective-permute-start | bytes 786440 | tf_op jit(solution)/shard_map/ppermute | solution.py:40
  209.9 11.4 %collective-permute-start.11 = (bf16[512,256]{0,1:T(8,128)(2,1)S(1)}, bf16[512,256]{0,1:T(8,128)(2,1)S(1)}, u32[]{:S(2)}, u32[]{:S(2)}) collective-permute-start(bf16[512,256]{0,1:T(8,128)(2,1)S(1)} %all_gather.15), channel_id=1, source_target_pairs={{0,1},{1,2},{2,3},{3,4},{4,5},{5,6},{6,7},{7,0},{8,9},{9,10},{10,1... | collective-permute-start | bytes 786440 | tf_op jit(solution)/shard_map/ppermute | solution.py:38
Sparse Core Ops, SparseCore 0:
  131.8 17.7 reduce-scatter.1
